TPU v7x, 32 devices: a whole 2x2x4 slice. The times are simulated.
32 devices in a mesh: dp: 8 (over z, x), tensor: 4 (over y, core).
Axes of the slice: x: 2, y: 2, z: 4, core: 2. Of those that a mesh axis runs over, the one named last changes fastest.
Arguments:
- layer_input: bfloat16 [16, 512, 2048], P('dp'), may hold values from -6 to 6
- segments: int32 [16, 512], P('dp'), may hold values from 0 to 3, never falling along the last dimension, each value on 1 to 256 neighbouring positions
- query_weight: bfloat16 [2048, 2048], P('dp', 'tensor'), may hold values from -0.125 to 0.125
- key_matrix: bfloat16 [2048, 1024], P('dp', 'tensor'), may hold values from -0.125 to 0.125
- value_matrix: bfloat16 [2048, 1024], P('dp', 'tensor'), may hold values from -0.125 to 0.125
- gate_weight: bfloat16 [2048, 2048], P('dp', 'tensor'), may hold values from -0.125 to 0.125
- out_weight: bfloat16 [2048, 2048], P('tensor', 'dp'), may hold values from -1 to 1
- ffn_gate_weight: bfloat16 [2048, 6144], P('dp', 'tensor'), may hold values from -0.125 to 0.125
- ffn_up_weight: bfloat16 [2048, 6144], P('dp', 'tensor'), may hold values from -0.125 to 0.125
- ffn_down_weight: bfloat16 [6144, 2048], P('tensor', 'dp'), may hold values from -0.109375 to 0.109375
- attn_gain: float32 [2048], replicated, may hold values from 0.5 to 1.5
- ffn_gain: float32 [2048], replicated, may hold values from 0.5 to 1.5
- query_gain: float32 [128], replicated, may hold values from 0.1 to 1.9
- key_norm_gain: float32 [128], replicated, may hold values from 0.1 to 1.9
- cotangent: bfloat16 [16, 512, 2048], P('dp'), may hold values from -6 to 6
Outputs:
- output: bfloat16 [16, 512, 2048], P('dp')
- input_grad: float32 [16, 512, 2048], P('dp')
- grad_query_weight: float32 [2048, 2048], P('dp', 'tensor')
- grad_key_weight: float32 [2048, 1024], P('dp', 'tensor')
- grad_value_weight: float32 [2048, 1024], P('dp', 'tensor')
- grad_gate_weight: float32 [2048, 2048], P('dp', 'tensor')
- grad_out_weight: float32 [2048, 2048], P('tensor', 'dp')
- grad_ffn_gate_weight: float32 [2048, 6144], P('dp', 'tensor')
- grad_ffn_up_weight: float32 [2048, 6144], P('dp', 'tensor')
- grad_ffn_down_weight: float32 [6144, 2048], P('tensor', 'dp')
- grad_attn_gain: float32 [2048], replicated
- grad_ffn_gain: float32 [2048], replicated
- grad_query_gain: float32 [128], replicated
- grad_key_gain: float32 [128], replicated
Inputs may be any that keep to these rules, and one draw needn't show every extreme that they name: `segments`: segment numbers never fall along a sequence; each document holds 1 to 256 tokens and some document holds exactly 256.
All inputs are finite; a program needn't handle non-finite values.
Results may differ from a plain program's by a relative error of at most 0.02.
Values may be sent and summed in bfloat16 or wider, within the bound.
No kernel may reach another device: no remote copies, remote signals or barrier semaphores. Data moves between devices by JAX's collectives and lax.ppermute only.
A program may use at most 256 MiB of HBM per device.

v0:
```python
import math
import jax
import jax.numpy as jnp
from jax import lax
from jax.sharding import PartitionSpec as P

epsilon = 1e-06


def norm_fwd(vector_in):
    scale_inv = lax.rsqrt(jnp.mean(vector_in * vector_in, axis=-1, keepdims=True) + epsilon)
    return (vector_in * scale_inv, scale_inv)


def norm_back(normal, scale_inv, gain_vec, grad_in_rows, tensor_rank, share_rows):
    scaled = grad_in_rows * gain_vec
    grad_rows = scale_inv * (scaled - normal * jnp.mean(scaled * normal, axis=-1, keepdims=True))
    grad_gain = jnp.sum(
        lax.dynamic_slice_in_dim(grad_in_rows * normal, tensor_rank * share_rows, share_rows, 0),
        axis=0,
    )
    return (grad_rows, grad_gain)


def rotary_apply(vector_in, cosine_table, sine_table):
    halfway = vector_in.shape[-1] // 2
    turned = jnp.concatenate([-vector_in[..., halfway:], vector_in[..., :halfway]], axis=-1)
    return vector_in * cosine_table + turned * sine_table


def tables(segment_row, head_size):
    token_length = segment_row.shape[0]
    places = jnp.arange(token_length, dtype=jnp.int32)
    changed = jnp.concatenate(
        [jnp.ones((1,), dtype=jnp.bool_), segment_row[1:] != segment_row[:-1]]
    )
    starts = lax.cummax(jnp.where(changed, places, jnp.zeros_like(places)), axis=0)
    position = (places - starts).astype(jnp.float32)
    frequency = jnp.exp(
        jnp.arange(head_size // 2, dtype=jnp.float32) * (-2.0 * math.log(1000000.0) / head_size)
    )
    angles = position[:, None] * frequency[None, :]
    angles = jnp.concatenate([angles, angles], axis=-1)
    allowed = (segment_row[:, None] == segment_row[None, :]) & (places[None, :] <= places[:, None])
    return (jnp.cos(angles)[:, None, :], jnp.sin(angles)[:, None, :], allowed)


def layer_pass(
    seq_input,
    seg_row,
    grad_out,
    gathered,
    attn_gain,
    ffn_gain,
    query_gain,
    key_norm_gain,
    tensor_rank,
    share_rows,
):
    full_q, full_k, full_v, full_g, full_o, full_gf, full_up, full_dn = gathered
    head_size = query_gain.shape[0]
    token_length = seq_input.shape[0]
    heads_q = full_q.shape[1] // head_size
    heads_kv = full_k.shape[1] // head_size
    group_width = heads_q // heads_kv
    scaling = head_size ** (-0.5)
    low_type = jnp.bfloat16
    wide_type = jnp.float32
    cosine_table, sine_table, allowed = tables(seg_row, head_size)
    normal_one, inv_one = norm_fwd(seq_input)
    first_normed = (normal_one * attn_gain).astype(low_type)
    query_proj = jnp.dot(first_normed, full_q, preferred_element_type=wide_type)
    key_projected = jnp.dot(first_normed, full_k, preferred_element_type=wide_type)
    value_projected = jnp.dot(first_normed, full_v, preferred_element_type=wide_type)
    gate_proj = jnp.dot(first_normed, full_g, preferred_element_type=wide_type)

    def prepare(query_in, key_in, gain_q, gain_k):
        query_n = norm_fwd(query_in.reshape(token_length, heads_q, head_size))[0] * gain_q
        key_n = norm_fwd(key_in.reshape(token_length, heads_kv, head_size))[0] * gain_k
        return (
            rotary_apply(query_n, cosine_table, sine_table),
            rotary_apply(key_n, cosine_table, sine_table),
        )

    (query_full, key_full), prepare_back = jax.vjp(
        prepare, query_proj, key_projected, query_gain, key_norm_gain
    )
    query_low = query_full.astype(low_type).reshape(token_length, heads_kv, group_width, head_size)
    key_low = key_full.astype(low_type)
    value_low = value_projected.astype(low_type).reshape(token_length, heads_kv, head_size)
    raw_scores = jnp.einsum("skgd,tkd->kgst", query_low, key_low, preferred_element_type=wide_type)
    scores = jnp.where(allowed, raw_scores * scaling, -1000000000.0)
    highest = jnp.max(scores, axis=-1, keepdims=True)
    exponent = jnp.exp(scores - highest)
    row_total = jnp.sum(exponent, axis=-1, keepdims=True)
    softmaxed = exponent / row_total
    log_total = highest + jnp.log(row_total)
    attended = jnp.einsum(
        "kgst,tkd->skgd", softmaxed.astype(low_type), value_low, preferred_element_type=wide_type
    ).reshape(token_length, heads_q * head_size)
    gate_sig = jax.nn.sigmoid(gate_proj)
    gated = (attended * gate_sig).astype(low_type)
    branch_one = lax.psum(jnp.dot(gated, full_o, preferred_element_type=wide_type), "tensor")
    middle = seq_input + branch_one
    normal_two, inv_two = norm_fwd(middle)
    second_normed = (normal_two * ffn_gain).astype(low_type)
    ffn_gate = jnp.dot(second_normed, full_gf, preferred_element_type=wide_type)
    ffn_up = jnp.dot(second_normed, full_up, preferred_element_type=wide_type)
    sig_gate = jax.nn.sigmoid(ffn_gate)
    active = ffn_gate * sig_gate
    hidden = (active * ffn_up).astype(low_type)
    branch_two = lax.psum(
        jnp.dot(hidden, full_dn, preferred_element_type=wide_type).astype(jnp.bfloat16), "tensor"
    ).astype(jnp.float32)
    result = (middle + branch_two).astype(low_type)
    grad_low = grad_out.astype(low_type)
    grad_dn = jnp.einsum("sf,sd->fd", hidden, grad_low, preferred_element_type=wide_type)
    grad_hidden = jnp.einsum("sd,fd->sf", grad_low, full_dn, preferred_element_type=wide_type)
    grad_ffn_gate = (grad_hidden * ffn_up * sig_gate * (1.0 + ffn_gate * (1.0 - sig_gate))).astype(
        low_type
    )
    grad_ffn_up = (grad_hidden * active).astype(low_type)
    grad_gf = jnp.einsum(
        "sd,sf->df", second_normed, grad_ffn_gate, preferred_element_type=wide_type
    )
    grad_up = jnp.einsum("sd,sf->df", second_normed, grad_ffn_up, preferred_element_type=wide_type)
    part_two = jnp.einsum(
        "sf,df->sd", grad_ffn_gate, full_gf, preferred_element_type=wide_type
    ) + jnp.einsum("sf,df->sd", grad_ffn_up, full_up, preferred_element_type=wide_type)
    grad_second = lax.psum(part_two, "tensor")
    back_two, grad_ffn_gain = norm_back(
        normal_two, inv_two, ffn_gain, grad_second, tensor_rank, share_rows
    )
    grad_middle = grad_out + back_two
    middle_low = grad_middle.astype(low_type)
    grad_o = jnp.einsum("sf,sd->fd", gated, middle_low, preferred_element_type=wide_type)
    grad_gated = (
        jnp.einsum("sd,fd->sf", middle_low, full_o, preferred_element_type=wide_type)
        .astype(low_type)
        .astype(wide_type)
    )
    grad_attended = (
        (grad_gated * gate_sig)
        .astype(low_type)
        .reshape(token_length, heads_kv, group_width, head_size)
    )
    grad_gate_proj = (grad_gated * attended * gate_sig * (1.0 - gate_sig)).astype(low_type)
    raw_again = jnp.einsum("skgd,tkd->kgst", query_low, key_low, preferred_element_type=wide_type)
    probs_again = jnp.exp(jnp.where(allowed, raw_again * scaling, -1000000000.0) - log_total)
    grad_value = (
        jnp.einsum(
            "kgst,skgd->tkd",
            probs_again.astype(low_type),
            grad_attended,
            preferred_element_type=wide_type,
        )
        .astype(low_type)
        .reshape(token_length, heads_kv * head_size)
    )
    grad_probs = jnp.einsum(
        "skgd,tkd->kgst", grad_attended, value_low, preferred_element_type=wide_type
    )
    grad_scores = (
        probs_again
        * (grad_probs - jnp.sum(probs_again * grad_probs, axis=-1, keepdims=True))
        * scaling
    ).astype(low_type)
    grad_queries = jnp.einsum(
        "kgst,tkd->skgd", grad_scores, key_low, preferred_element_type=wide_type
    ).reshape(token_length, heads_q, head_size)
    grad_keys = jnp.einsum(
        "kgst,skgd->tkd", grad_scores, query_low, preferred_element_type=wide_type
    )
    grad_query_proj, grad_key_proj, grad_query_gain, grad_key_gain = prepare_back(
        (grad_queries, grad_keys)
    )
    grad_query_low = grad_query_proj.astype(low_type)
    grad_key_low = grad_key_proj.astype(low_type)
    grad_q = jnp.einsum("sd,sf->df", first_normed, grad_query_low, preferred_element_type=wide_type)
    grad_k = jnp.einsum("sd,sf->df", first_normed, grad_key_low, preferred_element_type=wide_type)
    grad_v = jnp.einsum("sd,sf->df", first_normed, grad_value, preferred_element_type=wide_type)
    grad_g = jnp.einsum("sd,sf->df", first_normed, grad_gate_proj, preferred_element_type=wide_type)
    part_one = (
        jnp.einsum("sf,df->sd", grad_query_low, full_q, preferred_element_type=wide_type)
        + jnp.einsum("sf,df->sd", grad_key_low, full_k, preferred_element_type=wide_type)
        + jnp.einsum("sf,df->sd", grad_value, full_v, preferred_element_type=wide_type)
        + jnp.einsum("sf,df->sd", grad_gate_proj, full_g, preferred_element_type=wide_type)
    )
    grad_first = lax.psum(part_one.astype(jnp.bfloat16), "tensor").astype(jnp.float32)
    back_one, grad_attn_gain = norm_back(
        normal_one, inv_one, attn_gain, grad_first, tensor_rank, share_rows
    )
    grad_input = grad_middle + back_one
    return (
        result,
        grad_input,
        (grad_q, grad_k, grad_v, grad_g, grad_o, grad_gf, grad_up, grad_dn),
        (grad_attn_gain, grad_ffn_gain, grad_query_gain, grad_key_gain),
    )


def shards(
    layer_input,
    segments,
    query_weight,
    key_matrix,
    value_matrix,
    gate_weight,
    out_weight,
    ffn_gate_weight,
    ffn_up_weight,
    ffn_down_weight,
    attn_gain,
    ffn_gain,
    query_gain,
    key_norm_gain,
    cotangent,
):
    tensor_rank = lax.axis_index("tensor")
    share_rows = layer_input.shape[1] // lax.axis_size("tensor")
    gathered = (
        query_weight,
        key_matrix,
        value_matrix,
        gate_weight,
        out_weight,
        ffn_gate_weight,
        ffn_up_weight,
        ffn_down_weight,
    )
    totals = None
    gain_totals = (
        jnp.zeros_like(attn_gain),
        jnp.zeros_like(ffn_gain),
        jnp.zeros_like(query_gain),
        jnp.zeros_like(key_norm_gain),
    )
    results = []
    input_grads = []
    for micro_step in range(layer_input.shape[0]):
        gathered = (
            lax.all_gather(query_weight, "dp", axis=0, tiled=True),
            lax.all_gather(key_matrix, "dp", axis=0, tiled=True),
            lax.all_gather(value_matrix, "dp", axis=0, tiled=True),
            lax.all_gather(gate_weight, "dp", axis=0, tiled=True),
            lax.all_gather(out_weight, "dp", axis=1, tiled=True),
            lax.all_gather(ffn_gate_weight, "dp", axis=0, tiled=True),
            lax.all_gather(ffn_up_weight, "dp", axis=0, tiled=True),
            lax.all_gather(ffn_down_weight, "dp", axis=1, tiled=True),
        )
        result, grad_input, grads, gain_grads = layer_pass(
            layer_input[micro_step].astype(jnp.float32),
            segments[micro_step],
            cotangent[micro_step].astype(jnp.float32),
            gathered,
            attn_gain,
            ffn_gain,
            query_gain,
            key_norm_gain,
            tensor_rank,
            share_rows,
        )
        if totals is None:
            totals = grads
        else:
            totals = tuple((running + adding for running, adding in zip(totals, grads)))
        gain_totals = tuple((running + adding for running, adding in zip(gain_totals, gain_grads)))
        results.append(result)
        input_grads.append(grad_input)
    totals = (
        lax.psum_scatter(
            totals[0].astype(jnp.bfloat16), "dp", scatter_dimension=0, tiled=True
        ).astype(jnp.float32),
        lax.psum_scatter(
            totals[1].astype(jnp.bfloat16), "dp", scatter_dimension=0, tiled=True
        ).astype(jnp.float32),
        lax.psum_scatter(
            totals[2].astype(jnp.bfloat16), "dp", scatter_dimension=0, tiled=True
        ).astype(jnp.float32),
        lax.psum_scatter(
            totals[3].astype(jnp.bfloat16), "dp", scatter_dimension=0, tiled=True
        ).astype(jnp.float32),
        lax.psum_scatter(
            totals[4].astype(jnp.bfloat16), "dp", scatter_dimension=1, tiled=True
        ).astype(jnp.float32),
        lax.psum_scatter(
            totals[5].astype(jnp.bfloat16), "dp", scatter_dimension=0, tiled=True
        ).astype(jnp.float32),
        lax.psum_scatter(
            totals[6].astype(jnp.bfloat16), "dp", scatter_dimension=0, tiled=True
        ).astype(jnp.float32),
        lax.psum_scatter(
            totals[7].astype(jnp.bfloat16), "dp", scatter_dimension=1, tiled=True
        ).astype(jnp.float32),
    )
    sum_attn_gain, sum_ffn_gain, sum_query_gain, sum_key_gain = lax.psum(
        gain_totals, ("dp", "tensor")
    )
    return (
        jnp.stack(results),
        jnp.stack(input_grads),
        totals[0],
        totals[1],
        totals[2],
        totals[3],
        totals[4],
        totals[5],
        totals[6],
        totals[7],
        sum_attn_gain,
        sum_ffn_gain,
        sum_query_gain,
        sum_key_gain,
    )


def solution(mesh):
    return jax.shard_map(
        shards,
        mesh=mesh,
        in_specs=(
            P("dp", None, None),
            P("dp", None),
            P("dp", "tensor"),
            P("dp", "tensor"),
            P("dp", "tensor"),
            P("dp", "tensor"),
            P("tensor", "dp"),
            P("dp", "tensor"),
            P("dp", "tensor"),
            P("tensor", "dp"),
            P(),
            P(),
            P(),
            P(),
            P("dp", None, None),
        ),
        out_specs=(
            P("dp", None, None),
            P("dp", None, None),
            P("dp", "tensor"),
            P("dp", "tensor"),
            P("dp", "tensor"),
            P("dp", "tensor"),
            P("tensor", "dp"),
            P("dp", "tensor"),
            P("dp", "tensor"),
            P("tensor", "dp"),
            P(),
            P(),
            P(),
            P(),
        ),
        check_vma=False,
    )
```

profile of v0, /device:TPU:0, one launch (start us, length us, event | category | flops | bytes accessed | tf_op | source)
XLA Modules:
  0.0 1850.4 jit_solution(13215816996098095445)
XLA Ops:
  19.3 33.9 %all-gather.11.cloned.1.call-done = bf16[2048,256]{1,0:T(8,128)(2,1)} async-done(((bf16[256,256]{1,0:T(8,128)(2,1)}), bf16[2048,256]{1,0:T(8,128)(2,1)}) %all-gather.11.cloned.1.call-update) | async-done | bytes 1048592 | tf_op jit(solution)/shard_map/all_gather | solution.py:243
  59.6 34.7 %all-gather.9.cloned.1.call-done = bf16[2048,256]{1,0:T(8,128)(2,1)} async-done(((bf16[256,256]{1,0:T(8,128)(2,1)}), bf16[2048,256]{1,0:T(8,128)(2,1)}) %all-gather.9.cloned.1.call-update) | async-done | bytes 1048592 | tf_op jit(solution)/shard_map/all_gather | solution.py:244
  98.7 45.6 %all-gather.13.cloned.1.call-done = bf16[2048,512]{1,0:T(8,128)(2,1)} async-done(((bf16[256,512]{1,0:T(8,128)(2,1)}), bf16[2048,512]{1,0:T(8,128)(2,1)}) %all-gather.13.cloned.1.call-update) | async-done | bytes 2097168 | tf_op jit(solution)/shard_map/all_gather | solution.py:242
  162.4 31.5 %all-gather.15.cloned.1.call-done = bf16[2048,512]{1,0:T(8,128)(2,1)} async-done(((bf16[256,512]{1,0:T(8,128)(2,1)}), bf16[2048,512]{1,0:T(8,128)(2,1)}) %all-gather.15.cloned.1.call-update) | async-done | bytes 2097168 | tf_op jit(solution)/shard_map/all_gather | solution.py:245
  204.9 39.8 %all-gather.17.cloned.1.call-done = bf16[512,2048]{1,0:T(8,128)(2,1)} async-done(((bf16[512,256]{1,0:T(8,128)(2,1)}), bf16[512,2048]{1,0:T(8,128)(2,1)}) %all-gather.17.cloned.1.call-update) | async-done | bytes 2097168 | tf_op jit(solution)/shard_map/all_gather | solution.py:246
  255.5 148.9 %all-reduce.18.cloned.1.call-done = (f32[512,2048]{1,0:T(8,128)}, f32[512,2048]{1,0:T(8,128)}) async-done(((f32[512,2048]{1,0:T(8,128)}, f32[512,2048]{1,0:T(8,128)}), (f32[512,2048]{1,0:T(8,128)}, f32[512,2048]{1,0:T(8,128)})) %all-reduce.18.cloned.1.call-update) | async-done | bytes 8388624 | tf_op jit(solution)/shard_map/psum | solution.py:103
  418.1 87.4 %all-gather.21.cloned.1.call-done = bf16[2048,1536]{1,0:T(8,128)(2,1)} async-done(((bf16[256,1536]{1,0:T(8,128)(2,1)}), bf16[2048,1536]{1,0:T(8,128)(2,1)}) %all-gather.21.cloned.1.call-update) | async-done | bytes 6291472 | tf_op jit(solution)/shard_map/all_gather | solution.py:248
  505.5 8.5 fusion.177
  514.0 90.6 %all-gather.19.cloned.1.call-done = bf16[2048,1536]{1,0:T(8,128)(2,1)} async-done(((bf16[256,1536]{1,0:T(8,128)(2,1)}), bf16[2048,1536]{1,0:T(8,128)(2,1)}) %all-gather.19.cloned.1.call-update) | async-done | bytes 6291472 | tf_op jit(solution)/shard_map/all_gather | solution.py:247
  604.6 8.6 fusion.176
  623.4 81.0 %all-gather.23.cloned.1.call-done = bf16[1536,2048]{1,0:T(8,128)(2,1)} async-done(((bf16[1536,256]{1,0:T(8,128)(2,1)}), bf16[1536,2048]{1,0:T(8,128)(2,1)}) %all-gather.23.cloned.1.call-update) | async-done | bytes 6291472 | tf_op jit(solution)/shard_map/all_gather | solution.py:249
  704.3 11.4 multiply_convert_fusion.4
  716.8 8.3 fusion.186
  725.1 7.7 multiply_convert_fusion.6
  739.6 7.9 convolution_add_fusion.1
  752.8 8.1 convolution_convert_fusion.1
  760.9 7.4 convolution_convert_fusion
  768.4 135.6 %all-reduce.16.cloned.1.call-done = (f32[512,2048]{1,0:T(8,128)}, f32[512,2048]{1,0:T(8,128)}) async-done(((f32[512,2048]{1,0:T(8,128)}, f32[512,2048]{1,0:T(8,128)}), (f32[512,2048]{1,0:T(8,128)}, f32[512,2048]{1,0:T(8,128)})) %all-reduce.16.cloned.1.call-update) | async-done | bytes 8388624 | tf_op jit(solution)/shard_map/psum | solution.py:130
  926.6 9.0 broadcast_multiply_fusion.2
  935.7 9.0 fusion.61
  953.7 9.1 broadcast_multiply_fusion.3
  962.8 9.3 fusion.67
  1065.0 43.2 %reduce-scatter.11.cloned.1.call-done = bf16[256,256]{1,0:T(8,128)(2,1)} async-done(((bf16[2048,256]{1,0:T(8,128)(2,1)}), bf16[256,256]{1,0:T(8,128)(2,1)}) %reduce-scatter.11.cloned.1.call-update) | async-done | bytes 131088 | tf_op jit(solution)/shard_map/reduce_scatter | solution.py:274
  1109.8 153.5 %all-reduce.20.cloned.1.call-done = (bf16[512,2048]{1,0:T(8,128)(2,1)}, bf16[512,2048]{1,0:T(8,128)(2,1)}, bf16[512,2048]{1,0:T(8,128)(2,1)}, bf16[512,2048]{1,0:T(8,128)(2,1)}) async-done(((bf16[512,2048]{1,0:T(8,128)(2,1)}, bf16[512,2048]{1,0:T(8,128)(2,1)}, bf16[512,2048]{1,0:T(8,128)(2,1)}, bf16[512,2048]{1,0:T(8,128)(2,1)}), (bf16[512,2048]{1,0:T(8,128)(2,1)}, bf16[512,2048]{1,0:T(8,128)(2,1)}, ...) | async-done | bytes 8388624 | tf_op jit(solution)/shard_map/psum | solution.py:112
  1273.9 17.2 add_bitcast_fusion.1
  1294.6 41.1 %reduce-scatter.17.cloned.1.call-done = bf16[512,256]{1,0:T(8,128)(2,1)} async-done(((bf16[512,2048]{1,0:T(8,128)(2,1)}), bf16[512,256]{1,0:T(8,128)(2,1)}) %reduce-scatter.17.cloned.1.call-update) | async-done | bytes 262160 | tf_op jit(solution)/shard_map/reduce_scatter | solution.py:283
  1337.5 69.2 %reduce-scatter.9.cloned.1.call-done = bf16[256,512]{1,0:T(8,128)(2,1)} async-done(((bf16[2048,512]{1,0:T(8,128)(2,1)}), bf16[256,512]{1,0:T(8,128)(2,1)}) %reduce-scatter.9.cloned.1.call-update) | async-done | bytes 262160 | tf_op jit(solution)/shard_map/reduce_scatter | solution.py:271
  1408.5 69.0 %reduce-scatter.15.cloned.1.call-done = bf16[256,512]{1,0:T(8,128)(2,1)} async-done(((bf16[2048,512]{1,0:T(8,128)(2,1)}), bf16[256,512]{1,0:T(8,128)(2,1)}) %reduce-scatter.15.cloned.1.call-update) | async-done | bytes 262160 | tf_op jit(solution)/shard_map/reduce_scatter | solution.py:280
  1479.3 43.3 %all-reduce.8 = (f32[2048]{0:T(1024)}, f32[2048]{0:T(1024)}, f32[128]{0:T(128)}, f32[128]{0:T(128)}) all-reduce(f32[2048]{0:T(1024)S(1)} %add.311, f32[2048]{0:T(1024)S(1)} %add.312, f32[128]{0:T(128)S(1)} %add.313, f32[128]{0:T(128)S(1)} %add.314), channel_id=1, replica_groups=mesh['dp'=8,'tensor'=4] {'dp','tensor'}, use_global_device_ids=true, to_apply=%region_44.45 | all-reduce | flops 4352 | bytes 34816 | tf_op jit(solution)/shard_map/psum | solution.py:296
  1532.2 66.7 %reduce-scatter.21.cloned.1.call-done = bf16[256,1536]{1,0:T(8,128)(2,1)} async-done(((bf16[2048,1536]{1,0:T(8,128)(2,1)}), bf16[256,1536]{1,0:T(8,128)(2,1)}) %reduce-scatter.21.cloned.1.call-update) | async-done | bytes 786448 | tf_op jit(solution)/shard_map/reduce_scatter | solution.py:289
  1601.4 118.3 %reduce-scatter.19.cloned.1.call-done = bf16[256,1536]{1,0:T(8,128)(2,1)} async-done(((bf16[2048,1536]{1,0:T(8,128)(2,1)}), bf16[256,1536]{1,0:T(8,128)(2,1)}) %reduce-scatter.19.cloned.1.call-update) | async-done | bytes 786448 | tf_op jit(solution)/shard_map/reduce_scatter | solution.py:286
  1722.2 118.9 %reduce-scatter.23.cloned.1.call-done = bf16[1536,256]{1,0:T(8,128)(2,1)} async-done(((bf16[1536,2048]{1,0:T(8,128)(2,1)}), bf16[1536,256]{1,0:T(8,128)(2,1)}) %reduce-scatter.23.cloned.1.call-update) | async-done | bytes 786448 | tf_op jit(solution)/shard_map/reduce_scatter | solution.py:292
  (451 shorter events, 260.7 us)
Async XLA Ops:
  7.2 46.0 %all-gather.11.cloned.1.call-start = ((), (), s32[]{:S(2)}) async-start(), calls=%async_computation.9 | async-start | bytes 1179648 | tf_op jit(solution)/shard_map/all_gather | solution.py:243
  7.9 86.4 %all-gather.9.cloned.1.call-start = ((), (), s32[]{:S(2)}) async-start(), calls=%async_computation.8 | async-start | bytes 1179648 | tf_op jit(solution)/shard_map/all_gather | solution.py:244
  8.7 135.6 %all-gather.13.cloned.1.call-start = ((), (), s32[]{:S(2)}) async-start(), calls=%async_computation.10 | async-start | bytes 2359296 | tf_op jit(solution)/shard_map/all_gather | solution.py:242
  9.4 184.5 %all-gather.15.cloned.1.call-start = ((), (), s32[]{:S(2)}) async-start(), calls=%async_computation.11 | async-start | bytes 2359296 | tf_op jit(solution)/shard_map/all_gather | solution.py:245
  10.0 234.7 %all-gather.17.cloned.1.call-start = ((), (), s32[]{:S(2)}) async-start(), calls=%async_computation.12 | async-start | bytes 2359296 | tf_op jit(solution)/shard_map/all_gather | solution.py:246
  10.6 393.9 %all-reduce.18.cloned.1.call-start = ((), (), s32[]{:S(2)}) async-start(), calls=%async_computation.25 | async-start | bytes 16777216 | tf_op jit(solution)/shard_map/psum | solution.py:103
  18.2 138.5 %copy-start.36 = (f32[512,128]{0,1:T(8,128)}, f32[512,128]{0,1:T(8,128)S(1)}, u32[]{:S(2)}) copy-start(f32[512,128]{0,1:T(8,128)S(1)} %get-tuple-element.88) | copy-start | bytes 786436
  18.2 138.5 %copy-start.48 = (f32[512,128]{0,1:T(8,128)}, f32[512,128]{0,1:T(8,128)S(1)}, u32[]{:S(2)}) copy-start(f32[512,128]{0,1:T(8,128)S(1)} %get-tuple-element.89) | copy-start | bytes 786436
  19.2 136.1 %copy-start.38 = (f32[512,128]{0,1:T(8,128)}, f32[512,128]{0,1:T(8,128)S(1)}, u32[]{:S(2)}) copy-start(f32[512,128]{0,1:T(8,128)S(1)} %get-tuple-element.90) | copy-start | bytes 786436
  19.2 136.1 %copy-start.46 = (f32[512,128]{0,1:T(8,128)}, f32[512,128]{0,1:T(8,128)S(1)}, u32[]{:S(2)}) copy-start(f32[512,128]{0,1:T(8,128)S(1)} %get-tuple-element.91) | copy-start | bytes 786436
  19.3 174.6 %copy-start.113 = (f32[512]{0:T(512)}, f32[512]{0:T(512)S(1)}, u32[]{:S(2)}) copy-start(f32[512]{0:T(512)S(1)} %get-tuple-element.131) | copy-start | bytes 6148
  19.3 180.5 %copy-start.111 = (f32[512]{0:T(512)}, f32[512]{0:T(512)S(1)}, u32[]{:S(2)}) copy-start(f32[512]{0:T(512)S(1)} %get-tuple-element.130) | copy-start | bytes 6148
  59.4 98.3 %copy-start.86 = (bf16[512,2,128,1]{0,2,3,1:T(8,128)(2,1)}, bf16[512,2,128,1]{0,2,3,1:T(8,128)(2,1)S(1)}, u32[]{:S(2)}) copy-start(bf16[512,2,128,1]{0,2,3,1:T(8,128)(2,1)S(1)} %fusion.131) | copy-start | bytes 786436
  59.6 96.1 %copy-start.84 = (bf16[512,2,128,1]{0,2,3,1:T(8,128)(2,1)}, bf16[512,2,128,1]{0,2,3,1:T(8,128)(2,1)S(1)}, u32[]{:S(2)}) copy-start(bf16[512,2,128,1]{0,2,3,1:T(8,128)(2,1)S(1)} %fusion.132) | copy-start | bytes 786436
  97.7 101.1 %copy-start.94 = (bf16[512,256]{0,1:T(8,128)(2,1)}, bf16[512,256]{0,1:T(8,128)(2,1)S(1)}, u32[]{:S(2)}) copy-start(bf16[512,256]{0,1:T(8,128)(2,1)S(1)} %convolution_convert_fusion.4) | copy-start | bytes 786436
  98.7 62.8 %copy-start.92 = (bf16[512,256]{0,1:T(8,128)(2,1)}, bf16[512,256]{0,1:T(8,128)(2,1)S(1)}, u32[]{:S(2)}) copy-start(bf16[512,256]{0,1:T(8,128)(2,1)S(1)} %convolution_convert_fusion.5) | copy-start | bytes 786436
  198.8 51.1 %copy-start.62 = (bf16[512,512]{0,1:T(8,128)(2,1)}, bf16[512,512]{0,1:T(8,128)(2,1)S(1)}, u32[]{:S(2)}) copy-start(bf16[512,512]{0,1:T(8,128)(2,1)S(1)} %get-tuple-element.120) | copy-start | bytes 1572868
  204.9 48.3 %copy-start.76 = (bf16[512,512]{0,1:T(8,128)(2,1)}, bf16[512,512]{0,1:T(8,128)(2,1)S(1)}, u32[]{:S(2)}) copy-start(bf16[512,512]{0,1:T(8,128)(2,1)S(1)} %get-tuple-element.124) | copy-start | bytes 1572868
  253.2 252.3 %all-gather.21.cloned.1.call-start = ((), (), s32[]{:S(2)}) async-start(), calls=%async_computation.14 | async-start | bytes 7077888 | tf_op jit(solution)/shard_map/all_gather | solution.py:248
  254.0 350.6 %all-gather.19.cloned.1.call-start = ((), (), s32[]{:S(2)}) async-start(), calls=%async_computation.13 | async-start | bytes 7077888 | tf_op jit(solution)/shard_map/all_gather | solution.py:247
  254.7 449.6 %all-gather.23.cloned.1.call-start = ((), (), s32[]{:S(2)}) async-start(), calls=%async_computation.15 | async-start | bytes 7077888 | tf_op jit(solution)/shard_map/all_gather | solution.py:249
  255.5 648.5 %all-reduce.16.cloned.1.call-start = ((), (), s32[]{:S(2)}) async-start(), calls=%async_computation.24 | async-start | bytes 16777216 | tf_op jit(solution)/shard_map/psum | solution.py:130
  752.7 310.7 %reduce-scatter.13.cloned.1.call-start = ((), (), s32[]{:S(2)}) async-start(), calls=%async_computation.18 | async-start | bytes 1179648 | tf_op jit(solution)/shard_map/reduce_scatter | solution.py:277
  977.3 130.9 %reduce-scatter.11.cloned.1.call-start = ((), (), s32[]{:S(2)}) async-start(), calls=%async_computation.17 | async-start | bytes 1179648 | tf_op jit(solution)/shard_map/reduce_scatter | solution.py:274
  987.6 275.7 %all-reduce.20.cloned.1.call-start = ((), (), s32[]{:S(2)}) async-start(), calls=%async_computation.26 | async-start | bytes 16777216 | tf_op jit(solution)/shard_map/psum | solution.py:112
  1003.2 332.6 %reduce-scatter.17.cloned.1.call-start = ((), (), s32[]{:S(2)}) async-start(), calls=%async_computation.20 | async-start | bytes 2359296 | tf_op jit(solution)/shard_map/reduce_scatter | solution.py:283
  1010.5 396.2 %reduce-scatter.9.cloned.1.call-start = ((), (), s32[]{:S(2)}) async-start(), calls=%async_computation.16 | async-start | bytes 2359296 | tf_op jit(solution)/shard_map/reduce_scatter | solution.py:271
  1016.9 460.6 %reduce-scatter.15.cloned.1.call-start = ((), (), s32[]{:S(2)}) async-start(), calls=%async_computation.19 | async-start | bytes 2359296 | tf_op jit(solution)/shard_map/reduce_scatter | solution.py:280
  1023.1 575.8 %reduce-scatter.21.cloned.1.call-start = ((), (), s32[]{:S(2)}) async-start(), calls=%async_computation.22 | async-start | bytes 7077888 | tf_op jit(solution)/shard_map/reduce_scatter | solution.py:289
  1034.6 685.1 %reduce-scatter.19.cloned.1.call-start = ((), (), s32[]{:S(2)}) async-start(), calls=%async_computation.21 | async-start | bytes 7077888 | tf_op jit(solution)/shard_map/reduce_scatter | solution.py:286
  1046.1 795.0 %reduce-scatter.23.cloned.1.call-start = ((), (), s32[]{:S(2)}) async-start(), calls=%async_computation.23 | async-start | bytes 7077888 | tf_op jit(solution)/shard_map/reduce_scatter | solution.py:292
  1291.1 231.5 %copy-start.35 = (bf16[1,512,2048]{2,1,0:T(8,128)(2,1)S(1)}, bf16[1,512,2048]{2,1,0:T(8,128)(2,1)}, u32[]{:S(2)}) copy-start(bf16[1,512,2048]{2,1,0:T(8,128)(2,1)} %get-tuple-element.66) | copy-start | bytes 6291460
  (125 other events, 585.2 us)
Sparse Core Ops, SparseCore 0:
  10.1 42.9 all-gather.10
  55.3 38.9 all-gather.8
  96.4 47.7 all-gather.12
  146.3 47.6 all-gather.14
  195.8 48.8 all-gather.16
  253.4 151.0 all-reduce.17
  406.6 98.8 all-gather.20
  507.7 96.8 all-gather.18
  606.6 97.6 all-gather.22
  752.8 151.0 all-reduce.15
  977.4 64.3 reduce-scatter.12
  1045.0 63.1 reduce-scatter.10
  1111.4 151.8 all-reduce.19
  1266.7 68.9 reduce-scatter.16
  1339.1 67.5 reduce-scatter.8
  1410.1 67.3 reduce-scatter.14
  1480.9 117.9 reduce-scatter.20
  1602.4 117.2 reduce-scatter.18
  1723.3 117.7 reduce-scatter.22
where the time goes:
time: 1860 us; the launch traced here: 1850 us
  waiting for transfers between devices  1410 us (76%)
  matrix products  247 us (13%)
  other arithmetic  98.7 us (5%)
  blocking collectives  43.3 us (2%)
  local copies, waits for them, and re-layouts  30 us (2%)
    psum x1, waiting for transfers between devices, layer_pass(): lax.psum(jnp.dot(hidden, full_dn, preferred_element_type=wide_type).astyp...  154 us
    psum x1, waiting for transfers between devices, layer_pass(): lax.psum(jnp.dot(gated, full_o, preferred_element_type=wide_type), 'tensor')  149 us
    psum x1, waiting for transfers between devices, layer_pass(): grad_second = lax.psum(part_two, 'tensor')  136 us
    reduce_scatter x1, waiting for transfers between devices, shards(): lax.psum_scatter(totals[7].astype(jnp.bfloat16), 'dp', scatter_dimension=...  119 us
    reduce_scatter x1, waiting for transfers between devices, shards(): lax.psum_scatter(totals[5].astype(jnp.bfloat16), 'dp', scatter_dimension=...  118 us
    all_gather x1, waiting for transfers between devices, shards(): lax.all_gather(ffn_gate_weight, 'dp', axis=0, tiled=True)  90.6 us
    all_gather x1, waiting for transfers between devices, shards(): lax.all_gather(ffn_up_weight, 'dp', axis=0, tiled=True)  87.4 us
    all_gather x1, waiting for transfers between devices, shards(): lax.all_gather(ffn_down_weight, 'dp', axis=1, tiled=True)  81 us
  transfers between devices with their start and end apart: 19, of which 18 were waited for; matrix products, arithmetic and copies ran while one was open for 12% of the time, Pallas kernels for 0%

commit v1 on v0

--- a/solution.py
+++ b/solution.py
@@ -109,8 +109,12 @@
     sig_gate = jax.nn.sigmoid(ffn_gate)
     active = ffn_gate * sig_gate
     hidden = (active * ffn_up).astype(low_type)
-    branch_two = lax.psum(
-        jnp.dot(hidden, full_dn, preferred_element_type=wide_type).astype(jnp.bfloat16), "tensor"
+    branch_two = jnp.sum(
+        lax.all_gather(
+            jnp.dot(hidden, full_dn, preferred_element_type=wide_type).astype(jnp.bfloat16),
+            "tensor",
+        ),
+        axis=0,
     ).astype(jnp.float32)
     result = (middle + branch_two).astype(low_type)
     grad_low = grad_out.astype(low_type)

time: 1860 us -> 1920 us (1.032)
  waiting for transfers between devices: 1410 us -> 1470 us
    psum x1, waiting for transfers between devices: 154 us -> 0.02 us  [layer_pass(): lax.psum(part_one.astype(jnp.bfloat16), 'tensor').astype(jnp.float32)]
    all_gather x0 -> x2, waiting for transfers between devices: none -> 109 us  [layer_pass(): lax.all_gather(jnp.dot(hidden, full_dn, preferred_element_type=wide_type)...]
    reduce_scatter x1, waiting for transfers between devices: 0.02 us -> 60.5 us  [shards(): lax.psum_scatter(totals[2].astype(jnp.bfloat16), 'dp', scatter_dimension=...]
    reduce_scatter x1, waiting for transfers between devices: 119 us -> 67.1 us  [shards(): lax.psum_scatter(totals[7].astype(jnp.bfloat16), 'dp', scatter_dimension=...]
    reduce_scatter x1, waiting for transfers between devices: 66.7 us -> 92.1 us  [shards(): lax.psum_scatter(totals[6].astype(jnp.bfloat16), 'dp', scatter_dimension=...]
    reduce_scatter x1, waiting for transfers between devices: 41.1 us -> 65.9 us  [shards(): lax.psum_scatter(totals[4].astype(jnp.bfloat16), 'dp', scatter_dimension=...]
    reduce_scatter x1, waiting for transfers between devices: 43.2 us -> 65 us  [shards(): lax.psum_scatter(totals[1].astype(jnp.bfloat16), 'dp', scatter_dimension=...]
  transfers between devices with their start and end apart: 19 -> 21, of which waited for: 18 -> 20; matrix products, arithmetic and copies ran while one was open for 12% -> 12% of each run, Pallas kernels for 0% -> 0%
where the time goes in v1:
time: 1920 us
  waiting for transfers between devices  1470 us (77%)
  matrix products  249 us (13%)
  other arithmetic  114 us (6%)
  blocking collectives  43.2 us (2%)
  local copies, waits for them, and re-layouts  26.1 us (1%)
    psum x1, waiting for transfers between devices, layer_pass(): grad_second = lax.psum(part_two, 'tensor')  151 us
    psum x1, waiting for transfers between devices, layer_pass(): lax.psum(jnp.dot(gated, full_o, preferred_element_type=wide_type), 'tensor')  149 us
    reduce_scatter x1, waiting for transfers between devices, shards(): lax.psum_scatter(totals[5].astype(jnp.bfloat16), 'dp', scatter_dimension=...  119 us
    all_gather x2, waiting for transfers between devices, layer_pass(): lax.all_gather(jnp.dot(hidden, full_dn, preferred_element_type=wide_type)...  109 us
    reduce_scatter x1, waiting for transfers between devices, shards(): lax.psum_scatter(totals[6].astype(jnp.bfloat16), 'dp', scatter_dimension=...  92.1 us
    all_gather x1, waiting for transfers between devices, shards(): lax.all_gather(ffn_gate_weight, 'dp', axis=0, tiled=True)  90.6 us
    all_gather x1, waiting for transfers between devices, shards(): lax.all_gather(ffn_up_weight, 'dp', axis=0, tiled=True)  87.4 us
    all_gather x1, waiting for transfers between devices, shards(): lax.all_gather(ffn_down_weight, 'dp', axis=1, tiled=True)  80.8 us
  transfers between devices with their start and end apart: 21, of which 20 were waited for; matrix products, arithmetic and copies ran while one was open for 12% of the time, Pallas kernels for 0%

profile of v1, /device:TPU:0, one launch (start us, length us, event | category | flops | bytes accessed | tf_op | source)
XLA Modules:
  0.0 1917.3 jit_solution(16500278229862544576)
XLA Ops:
  19.3 33.9 %all-gather.15.cloned.1.call-done = bf16[2048,256]{1,0:T(8,128)(2,1)} async-done(((bf16[256,256]{1,0:T(8,128)(2,1)}), bf16[2048,256]{1,0:T(8,128)(2,1)}) %all-gather.15.cloned.1.call-update) | async-done | bytes 1048592 | tf_op jit(solution)/shard_map/all_gather | solution.py:247
  59.6 34.7 %all-gather.13.cloned.1.call-done = bf16[2048,256]{1,0:T(8,128)(2,1)} async-done(((bf16[256,256]{1,0:T(8,128)(2,1)}), bf16[2048,256]{1,0:T(8,128)(2,1)}) %all-gather.13.cloned.1.call-update) | async-done | bytes 1048592 | tf_op jit(solution)/shard_map/all_gather | solution.py:248
  98.7 45.6 %all-gather.17.cloned.1.call-done = bf16[2048,512]{1,0:T(8,128)(2,1)} async-done(((bf16[256,512]{1,0:T(8,128)(2,1)}), bf16[2048,512]{1,0:T(8,128)(2,1)}) %all-gather.17.cloned.1.call-update) | async-done | bytes 2097168 | tf_op jit(solution)/shard_map/all_gather | solution.py:246
  162.5 31.4 %all-gather.19.cloned.1.call-done = bf16[2048,512]{1,0:T(8,128)(2,1)} async-done(((bf16[256,512]{1,0:T(8,128)(2,1)}), bf16[2048,512]{1,0:T(8,128)(2,1)}) %all-gather.19.cloned.1.call-update) | async-done | bytes 2097168 | tf_op jit(solution)/shard_map/all_gather | solution.py:249
  205.0 39.8 %all-gather.21.cloned.1.call-done = bf16[512,2048]{1,0:T(8,128)(2,1)} async-done(((bf16[512,256]{1,0:T(8,128)(2,1)}), bf16[512,2048]{1,0:T(8,128)(2,1)}) %all-gather.21.cloned.1.call-update) | async-done | bytes 2097168 | tf_op jit(solution)/shard_map/all_gather | solution.py:250
  255.6 148.9 %all-reduce.18.cloned.1.call-done = (f32[512,2048]{1,0:T(8,128)}, f32[512,2048]{1,0:T(8,128)}) async-done(((f32[512,2048]{1,0:T(8,128)}, f32[512,2048]{1,0:T(8,128)}), (f32[512,2048]{1,0:T(8,128)}, f32[512,2048]{1,0:T(8,128)})) %all-reduce.18.cloned.1.call-update) | async-done | bytes 8388624 | tf_op jit(solution)/shard_map/psum | solution.py:103
  418.3 87.4 %all-gather.25.cloned.1.call-done = bf16[2048,1536]{1,0:T(8,128)(2,1)} async-done(((bf16[256,1536]{1,0:T(8,128)(2,1)}), bf16[2048,1536]{1,0:T(8,128)(2,1)}) %all-gather.25.cloned.1.call-update) | async-done | bytes 6291472 | tf_op jit(solution)/shard_map/all_gather | solution.py:252
  505.6 8.5 fusion.177
  514.1 90.6 %all-gather.23.cloned.1.call-done = bf16[2048,1536]{1,0:T(8,128)(2,1)} async-done(((bf16[256,1536]{1,0:T(8,128)(2,1)}), bf16[2048,1536]{1,0:T(8,128)(2,1)}) %all-gather.23.cloned.1.call-update) | async-done | bytes 6291472 | tf_op jit(solution)/shard_map/all_gather | solution.py:251
  604.7 8.6 fusion.176
  623.6 80.8 %all-gather.27.cloned.1.call-done = bf16[1536,2048]{1,0:T(8,128)(2,1)} async-done(((bf16[1536,256]{1,0:T(8,128)(2,1)}), bf16[1536,2048]{1,0:T(8,128)(2,1)}) %all-gather.27.cloned.1.call-update) | async-done | bytes 6291472 | tf_op jit(solution)/shard_map/all_gather | solution.py:253
  704.5 11.4 multiply_convert_fusion.4
  717.0 8.5 fusion.186
  740.0 7.9 convolution_add_fusion.1
  753.2 151.1 %all-reduce.16.cloned.1.call-done = (f32[512,2048]{1,0:T(8,128)}, f32[512,2048]{1,0:T(8,128)}) async-done(((f32[512,2048]{1,0:T(8,128)}, f32[512,2048]{1,0:T(8,128)}), (f32[512,2048]{1,0:T(8,128)}, f32[512,2048]{1,0:T(8,128)})) %all-reduce.16.cloned.1.call-update) | async-done | bytes 8388624 | tf_op jit(solution)/shard_map/psum | solution.py:134
  927.1 9.0 broadcast_multiply_fusion.3
  936.1 8.1 fusion.67
  954.1 9.0 broadcast_multiply_fusion.2
  963.1 8.2 fusion.61
  1020.8 8.2 convolution_convert_fusion.1
  1083.4 60.5 %reduce-scatter.13.cloned.1.call-done = bf16[256,256]{1,0:T(8,128)(2,1)} async-done(((bf16[2048,256]{1,0:T(8,128)(2,1)}), bf16[256,256]{1,0:T(8,128)(2,1)}) %reduce-scatter.13.cloned.1.call-update) | async-done | bytes 131088 | tf_op jit(solution)/shard_map/reduce_scatter | solution.py:281
  1145.6 65.0 %reduce-scatter.11.cloned.1.call-done = bf16[256,256]{1,0:T(8,128)(2,1)} async-done(((bf16[2048,256]{1,0:T(8,128)(2,1)}), bf16[256,256]{1,0:T(8,128)(2,1)}) %reduce-scatter.11.cloned.1.call-update) | async-done | bytes 131088 | tf_op jit(solution)/shard_map/reduce_scatter | solution.py:278
  1216.0 65.9 %reduce-scatter.17.cloned.1.call-done = bf16[512,256]{1,0:T(8,128)(2,1)} async-done(((bf16[512,2048]{1,0:T(8,128)(2,1)}), bf16[512,256]{1,0:T(8,128)(2,1)}) %reduce-scatter.17.cloned.1.call-update) | async-done | bytes 262160 | tf_op jit(solution)/shard_map/reduce_scatter | solution.py:287
  1283.7 69.3 %reduce-scatter.9.cloned.1.call-done = bf16[256,512]{1,0:T(8,128)(2,1)} async-done(((bf16[2048,512]{1,0:T(8,128)(2,1)}), bf16[256,512]{1,0:T(8,128)(2,1)}) %reduce-scatter.9.cloned.1.call-update) | async-done | bytes 262160 | tf_op jit(solution)/shard_map/reduce_scatter | solution.py:275
  1354.9 68.9 %reduce-scatter.15.cloned.1.call-done = bf16[256,512]{1,0:T(8,128)(2,1)} async-done(((bf16[2048,512]{1,0:T(8,128)(2,1)}), bf16[256,512]{1,0:T(8,128)(2,1)}) %reduce-scatter.15.cloned.1.call-update) | async-done | bytes 262160 | tf_op jit(solution)/shard_map/reduce_scatter | solution.py:284
  1425.6 56.9 %all-gather.29.cloned.1.call-done = bf16[2048,2048]{1,0:T(8,128)(2,1)} async-done(((bf16[512,2048]{1,0:T(8,128)(2,1)}), bf16[2048,2048]{1,0:T(8,128)(2,1)}) %all-gather.29.cloned.1.call-update) | async-done | bytes 8388624 | tf_op jit(solution)/shard_map/all_gather | solution.py:113
  1489.7 52.5 %all-gather.31.cloned.1.call-done = bf16[2048,2048]{1,0:T(8,128)(2,1)} async-done(((bf16[512,2048]{1,0:T(8,128)(2,1)}), bf16[2048,2048]{1,0:T(8,128)(2,1)}) %all-gather.31.cloned.1.call-update) | async-done | bytes 8388624 | tf_op jit(solution)/shard_map/all_gather | solution.py:113
  1549.5 18.8 add_bitcast_fusion.1
  1571.7 92.1 %reduce-scatter.21.cloned.1.call-done = bf16[256,1536]{1,0:T(8,128)(2,1)} async-done(((bf16[2048,1536]{1,0:T(8,128)(2,1)}), bf16[256,1536]{1,0:T(8,128)(2,1)}) %reduce-scatter.21.cloned.1.call-update) | async-done | bytes 786448 | tf_op jit(solution)/shard_map/reduce_scatter | solution.py:293
  1666.3 118.9 %reduce-scatter.19.cloned.1.call-done = bf16[256,1536]{1,0:T(8,128)(2,1)} async-done(((bf16[2048,1536]{1,0:T(8,128)(2,1)}), bf16[256,1536]{1,0:T(8,128)(2,1)}) %reduce-scatter.19.cloned.1.call-update) | async-done | bytes 786448 | tf_op jit(solution)/shard_map/reduce_scatter | solution.py:290
  1787.6 43.2 %all-reduce.8 = (f32[2048]{0:T(1024)}, f32[2048]{0:T(1024)}, f32[128]{0:T(128)}, f32[128]{0:T(128)}) all-reduce(f32[2048]{0:T(1024)S(1)} %add.307, f32[2048]{0:T(1024)S(1)} %add.308, f32[128]{0:T(128)S(1)} %add.309, f32[128]{0:T(128)S(1)} %add.310), channel_id=1, replica_groups=mesh['dp'=8,'tensor'=4] {'dp','tensor'}, use_global_device_ids=true, to_apply=%region_44.45 | all-reduce | flops 4352 | bytes 34816 | tf_op jit(solution)/shard_map/psum | solution.py:300
  1840.5 67.1 %reduce-scatter.23.cloned.1.call-done = bf16[1536,256]{1,0:T(8,128)(2,1)} async-done(((bf16[1536,2048]{1,0:T(8,128)(2,1)}), bf16[1536,256]{1,0:T(8,128)(2,1)}) %reduce-scatter.23.cloned.1.call-update) | async-done | bytes 786448 | tf_op jit(solution)/shard_map/reduce_scatter | solution.py:296
  (427 shorter events, 290.2 us)
Async XLA Ops:
  7.2 46.0 %all-gather.15.cloned.1.call-start = ((), (), s32[]{:S(2)}) async-start(), calls=%async_computation.9 | async-start | bytes 1179648 | tf_op jit(solution)/shard_map/all_gather | solution.py:247
  7.9 86.4 %all-gather.13.cloned.1.call-start = ((), (), s32[]{:S(2)}) async-start(), calls=%async_computation.8 | async-start | bytes 1179648 | tf_op jit(solution)/shard_map/all_gather | solution.py:248
  8.7 135.6 %all-gather.17.cloned.1.call-start = ((), (), s32[]{:S(2)}) async-start(), calls=%async_computation.10 | async-start | bytes 2359296 | tf_op jit(solution)/shard_map/all_gather | solution.py:246
  9.4 184.5 %all-gather.19.cloned.1.call-start = ((), (), s32[]{:S(2)}) async-start(), calls=%async_computation.11 | async-start | bytes 2359296 | tf_op jit(solution)/shard_map/all_gather | solution.py:249
  10.0 234.7 %all-gather.21.cloned.1.call-start = ((), (), s32[]{:S(2)}) async-start(), calls=%async_computation.12 | async-start | bytes 2359296 | tf_op jit(solution)/shard_map/all_gather | solution.py:250
  10.6 394.0 %all-reduce.18.cloned.1.call-start = ((), (), s32[]{:S(2)}) async-start(), calls=%async_computation.27 | async-start | bytes 16777216 | tf_op jit(solution)/shard_map/psum | solution.py:103
  18.2 138.5 %copy-start.34 = (f32[512,128]{0,1:T(8,128)}, f32[512,128]{0,1:T(8,128)S(1)}, u32[]{:S(2)}) copy-start(f32[512,128]{0,1:T(8,128)S(1)} %get-tuple-element.86) | copy-start | bytes 786436
  18.2 138.5 %copy-start.44 = (f32[512,128]{0,1:T(8,128)}, f32[512,128]{0,1:T(8,128)S(1)}, u32[]{:S(2)}) copy-start(f32[512,128]{0,1:T(8,128)S(1)} %get-tuple-element.87) | copy-start | bytes 786436
  19.2 136.2 %copy-start.36 = (f32[512,128]{0,1:T(8,128)}, f32[512,128]{0,1:T(8,128)S(1)}, u32[]{:S(2)}) copy-start(f32[512,128]{0,1:T(8,128)S(1)} %get-tuple-element.88) | copy-start | bytes 786436
  19.2 136.2 %copy-start.46 = (f32[512,128]{0,1:T(8,128)}, f32[512,128]{0,1:T(8,128)S(1)}, u32[]{:S(2)}) copy-start(f32[512,128]{0,1:T(8,128)S(1)} %get-tuple-element.89) | copy-start | bytes 786436
  19.3 174.6 %copy-start.98 = (f32[512]{0:T(512)}, f32[512]{0:T(512)S(1)}, u32[]{:S(2)}) copy-start(f32[512]{0:T(512)S(1)} %get-tuple-element.129) | copy-start | bytes 6148
  19.3 180.5 %copy-start.96 = (f32[512]{0:T(512)}, f32[512]{0:T(512)S(1)}, u32[]{:S(2)}) copy-start(f32[512]{0:T(512)S(1)} %get-tuple-element.128) | copy-start | bytes 6148
  59.4 98.4 %copy-start.73 = (bf16[512,2,128,1]{0,2,3,1:T(8,128)(2,1)}, bf16[512,2,128,1]{0,2,3,1:T(8,128)(2,1)S(1)}, u32[]{:S(2)}) copy-start(bf16[512,2,128,1]{0,2,3,1:T(8,128)(2,1)S(1)} %fusion.131) | copy-start | bytes 786436
  59.6 96.2 %copy-start.75 = (bf16[512,2,128,1]{0,2,3,1:T(8,128)(2,1)}, bf16[512,2,128,1]{0,2,3,1:T(8,128)(2,1)S(1)}, u32[]{:S(2)}) copy-start(bf16[512,2,128,1]{0,2,3,1:T(8,128)(2,1)S(1)} %fusion.132) | copy-start | bytes 786436
  97.7 101.1 %copy-start.79 = (bf16[512,256]{0,1:T(8,128)(2,1)}, bf16[512,256]{0,1:T(8,128)(2,1)S(1)}, u32[]{:S(2)}) copy-start(bf16[512,256]{0,1:T(8,128)(2,1)S(1)} %convolution_convert_fusion.4) | copy-start | bytes 786436
  198.8 51.2 %copy-start.52 = (bf16[512,512]{0,1:T(8,128)(2,1)}, bf16[512,512]{0,1:T(8,128)(2,1)S(1)}, u32[]{:S(2)}) copy-start(bf16[512,512]{0,1:T(8,128)(2,1)S(1)} %get-tuple-element.118) | copy-start | bytes 1572868
  253.4 252.3 %all-gather.25.cloned.1.call-start = ((), (), s32[]{:S(2)}) async-start(), calls=%async_computation.14 | async-start | bytes 7077888 | tf_op jit(solution)/shard_map/all_gather | solution.py:252
  254.1 350.6 %all-gather.23.cloned.1.call-start = ((), (), s32[]{:S(2)}) async-start(), calls=%async_computation.13 | async-start | bytes 7077888 | tf_op jit(solution)/shard_map/all_gather | solution.py:251
  254.9 449.6 %all-gather.27.cloned.1.call-start = ((), (), s32[]{:S(2)}) async-start(), calls=%async_computation.15 | async-start | bytes 7077888 | tf_op jit(solution)/shard_map/all_gather | solution.py:253
  255.6 648.7 %all-reduce.16.cloned.1.call-start = ((), (), s32[]{:S(2)}) async-start(), calls=%async_computation.26 | async-start | bytes 16777216 | tf_op jit(solution)/shard_map/psum | solution.py:134
  753.1 323.5 %all-reduce.20.cloned.1.call-start = ((), (), s32[]{:S(2)}) async-start(), calls=%async_computation.28 | async-start | bytes 8388608 | tf_op jit(solution)/shard_map/psum | solution.py:193
  990.6 153.4 %reduce-scatter.13.cloned.1.call-start = ((), (), s32[]{:S(2)}) async-start(), calls=%async_computation.18 | async-start | bytes 1179648 | tf_op jit(solution)/shard_map/reduce_scatter | solution.py:281
  996.3 214.2 %reduce-scatter.11.cloned.1.call-start = ((), (), s32[]{:S(2)}) async-start(), calls=%async_computation.17 | async-start | bytes 1179648 | tf_op jit(solution)/shard_map/reduce_scatter | solution.py:278
  1001.7 280.3 %reduce-scatter.17.cloned.1.call-start = ((), (), s32[]{:S(2)}) async-start(), calls=%async_computation.20 | async-start | bytes 2359296 | tf_op jit(solution)/shard_map/reduce_scatter | solution.py:287
  1008.1 345.0 %reduce-scatter.9.cloned.1.call-start = ((), (), s32[]{:S(2)}) async-start(), calls=%async_computation.16 | async-start | bytes 2359296 | tf_op jit(solution)/shard_map/reduce_scatter | solution.py:275
  1014.2 409.6 %reduce-scatter.15.cloned.1.call-start = ((), (), s32[]{:S(2)}) async-start(), calls=%async_computation.19 | async-start | bytes 2359296 | tf_op jit(solution)/shard_map/reduce_scatter | solution.py:284
  1020.8 461.8 %all-gather.29.cloned.1.call-start = ((), (), s32[]{:S(2)}) async-start(), calls=%async_computation.24 | async-start | bytes 10485760 | tf_op jit(solution)/shard_map/all_gather | solution.py:113
  1029.0 513.2 %all-gather.31.cloned.1.call-start = ((), (), s32[]{:S(2)}) async-start(), calls=%async_computation.25 | async-start | bytes 10485760 | tf_op jit(solution)/shard_map/all_gather | solution.py:113
  1036.6 627.3 %reduce-scatter.21.cloned.1.call-start = ((), (), s32[]{:S(2)}) async-start(), calls=%async_computation.22 | async-start | bytes 7077888 | tf_op jit(solution)/shard_map/reduce_scatter | solution.py:293
  1048.2 736.9 %reduce-scatter.19.cloned.1.call-start = ((), (), s32[]{:S(2)}) async-start(), calls=%async_computation.21 | async-start | bytes 7077888 | tf_op jit(solution)/shard_map/reduce_scatter | solution.py:290
  1060.0 847.6 %reduce-scatter.23.cloned.1.call-start = ((), (), s32[]{:S(2)}) async-start(), calls=%async_computation.23 | async-start | bytes 7077888 | tf_op jit(solution)/shard_map/reduce_scatter | solution.py:296
  1568.2 262.6 %copy-start.33 = (bf16[1,512,2048]{2,1,0:T(8,128)(2,1)S(1)}, bf16[1,512,2048]{2,1,0:T(8,128)(2,1)}, u32[]{:S(2)}) copy-start(bf16[1,512,2048]{2,1,0:T(8,128)(2,1)} %get-tuple-element.64) | copy-start | bytes 6291460
  (111 other events, 540.7 us)
Sparse Core Ops, SparseCore 0:
  10.1 42.9 all-gather.14
  55.3 38.9 all-gather.12
  96.4 47.7 all-gather.16
  146.3 47.6 all-gather.18
  195.8 48.8 all-gather.20
  253.5 151.0 all-reduce.17
  406.8 98.8 all-gather.24
  507.8 96.8 all-gather.22
  606.8 97.6 all-gather.26
  753.2 151.0 all-reduce.15
  990.7 85.6 all-reduce.19
  1079.6 64.3 reduce-scatter.12
  1147.4 63.1 reduce-scatter.10
  1213.9 67.9 reduce-scatter.16
  1285.3 67.6 reduce-scatter.8
  1356.5 67.2 reduce-scatter.14
  1425.2 57.2 all-gather.28
  1483.9 58.2 all-gather.30
  1545.8 117.9 reduce-scatter.20
  1667.9 117.2 reduce-scatter.18
  1788.8 118.7 reduce-scatter.22
